TPU v7x, 32 devices: a whole 2x2x4 slice. The times are simulated.
32 devices in a mesh: img: 4 (over z), ty: 4 (over y, core), tx: 2 (over x).
Axes of the slice: x: 2, y: 2, z: 4, core: 2. Of those that a mesh axis runs over, the one named last changes fastest.
Arguments:
- block_in: float32 [4, 64, 16, 1152], P('img', 'ty', 'tx'), may hold values from -6 to 6
- bucket: int32 [4], P('img'), may hold values from 0 to 31
- tile_anchor: int32 [4, 4, 2, 2], P('img', 'ty', 'tx'), may hold values from 0 to 255
- cond_table: float32 [32, 1152], replicated, may hold values from -6 to 6
- mod_weight: bfloat16 [1152, 6912], P(None, ('ty', 'tx')), may hold values from -0.1875 to 0.1875
- mod_bias: float32 [6912], P(('ty', 'tx')), may hold values from -3 to 3
- qkv_weight: bfloat16 [1152, 3456], replicated, may hold values from -0.1875 to 0.1875
- query_gain: float32 [72], replicated, may hold values from 0.5 to 1.5
- key_gain: float32 [72], replicated, may hold values from 0.5 to 1.5
- out_weight: bfloat16 [1152, 1152], replicated, may hold values from -3.5 to 3.5
- gate_up_weight: bfloat16 [1152, 6144], replicated, may hold values from -0.1875 to 0.1875
- down_weight: bfloat16 [3072, 1152], replicated, may hold values from -0.109375 to 0.109375
- cotangent: float32 [4, 64, 16, 1152], P('img', 'ty', 'tx'), may hold values from -6 to 6
Outputs:
- output: float32 [4, 64, 16, 1152], P('img', 'ty', 'tx')
- in_grad: float32 [4, 64, 16, 1152], P('img', 'ty', 'tx')
- table_grad: float32 [32, 1152], P(('ty', 'tx'), 'img')
- modw_grad: float32 [1152, 6912], P('img', ('ty', 'tx'))
- modb_grad: float32 [6912], P(('ty', 'tx'))
- qkv_grad: float32 [1152, 3456], P(('ty', 'tx'), 'img')
- qgain_grad: float32 [72], replicated
- kgain_grad: float32 [72], replicated
- outw_grad: float32 [1152, 1152], P(('ty', 'tx'), 'img')
- gateup_grad: float32 [1152, 6144], P(('ty', 'tx'), 'img')
- down_grad: float32 [3072, 1152], P(('ty', 'tx'), 'img')
All inputs are finite; a program needn't handle non-finite values.
Results may differ from a plain program's by a relative error of at most 0.017.
Values may be sent and summed in bfloat16 or wider, within the bound.
No kernel may reach another device: no remote copies, remote signals or barrier semaphores. Data moves between devices by JAX's collectives and lax.ppermute only.
A program may use at most 256 MiB of HBM per device.

v0:
```python
import math
import jax
import jax.numpy as jnp
from jax import lax
from jax.sharding import PartitionSpec as P

HEADS = 16
HD = 72
EPS = 1e-06
PRECISE = lax.Precision.HIGHEST


def normed(value):
    return value * lax.rsqrt(jnp.mean(value * value, axis=-1, keepdims=True) + EPS)


def norm_back(value, upstream):
    inverse = lax.rsqrt(jnp.mean(value * value, axis=-1, keepdims=True) + EPS)
    unit_value = value * inverse
    return inverse * (
        upstream - unit_value * jnp.mean(upstream * unit_value, axis=-1, keepdims=True)
    )


def rotate(value, tables, turning):
    row_cos, row_sin, col_cos, col_sin = tables
    quarter = value.shape[-1] // 4
    first = value[..., :quarter]
    second = value[..., quarter : 2 * quarter]
    third = value[..., 2 * quarter : 3 * quarter]
    fourth = value[..., 3 * quarter :]
    row_turn = turning * row_sin
    col_turn = turning * col_sin
    return jnp.concatenate(
        [
            first * row_cos - second * row_turn,
            second * row_cos + first * row_turn,
            third * col_cos - fourth * col_turn,
            fourth * col_cos + third * col_turn,
        ],
        axis=-1,
    )


def silu_slope(value):
    sigma = jax.nn.sigmoid(value)
    return sigma * (1.0 + value * (1.0 - sigma))


def product(left, right):
    return jnp.einsum("ik,kj->ij", left, right, preferred_element_type=jnp.float32)


def product_rt(left, right):
    return jnp.einsum("ik,jk->ij", left, right, preferred_element_type=jnp.float32)


def product_lt(left, right):
    return jnp.einsum("ki,kj->ij", left, right, preferred_element_type=jnp.float32)


def on_device(
    block_in,
    bucket,
    tile_anchor,
    cond_table,
    mod_weight,
    mod_bias,
    qkv_weight,
    query_gain,
    key_gain,
    out_weight,
    gate_up_weight,
    down_weight,
    cotangent,
):
    images, tile_rows, tile_cols, model_width = block_in.shape
    tokens = tile_rows * tile_cols
    all_rows = images * tokens
    head_count = HEADS
    head_size = HD
    score_scale = head_size ** (-0.5)
    hidden_units = down_weight.shape[0]
    onehot = (bucket[:, None] == jnp.arange(cond_table.shape[0], dtype=jnp.int32)[None, :]).astype(
        jnp.float32
    )
    condition = jnp.dot(onehot, cond_table, precision=PRECISE)
    cond_act = jax.nn.silu(condition).astype(jnp.bfloat16)
    mod_part = product(cond_act, mod_weight) + mod_bias[None, :]
    modulation = lax.all_gather(mod_part, ("ty", "tx"), axis=1, tiled=True)
    pieces = [
        modulation[:, None, index * model_width : (index + 1) * model_width] for index in range(6)
    ]
    shift_in, scale_in, gate_in, shift_mid, scale_mid, gate_mid = pieces
    places = jnp.arange(tokens, dtype=jnp.int32)
    row_pos = (tile_anchor[:, 0, 0, 0][:, None] + places[None, :] // tile_cols).astype(jnp.float32)
    col_pos = (tile_anchor[:, 0, 0, 1][:, None] + places[None, :] % tile_cols).astype(jnp.float32)
    quarter = head_size // 4
    frequency = jnp.exp(-math.log(10000.0) * jnp.arange(quarter, dtype=jnp.float32) / quarter)
    row_angle = row_pos[:, :, None, None] * frequency
    col_angle = col_pos[:, :, None, None] * frequency
    tables = (jnp.cos(row_angle), jnp.sin(row_angle), jnp.cos(col_angle), jnp.sin(col_angle))
    inputs = block_in.reshape(images, tokens, model_width)
    normed_in = normed(inputs)
    hidden_in = (
        (normed_in * (1.0 + scale_in) + shift_in)
        .astype(jnp.bfloat16)
        .reshape(all_rows, model_width)
    )
    qkv = product(hidden_in, qkv_weight).reshape(images, tokens, 3 * model_width)
    query_raw = qkv[..., :model_width].reshape(images, tokens, head_count, head_size)
    key_raw = qkv[..., model_width : 2 * model_width].reshape(images, tokens, head_count, head_size)
    query_unit = normed(query_raw)
    key_unit = normed(key_raw)
    query_low = rotate(query_unit * query_gain, tables, 1.0).astype(jnp.bfloat16)
    key_low = rotate(key_unit * key_gain, tables, 1.0).astype(jnp.bfloat16)
    value_low = qkv[..., 2 * model_width :].astype(jnp.bfloat16)
    keys_all, values_all = (
        lax.all_gather(
            key_low.reshape(images, tokens, model_width), ("ty", "tx"), axis=1, tiled=True
        ),
        lax.all_gather(value_low, ("ty", "tx"), axis=1, tiled=True),
    )
    key_heads = keys_all.reshape(images, -1, head_count, head_size)
    value_heads = values_all.reshape(images, -1, head_count, head_size)

    def attend(items):
        query_img, key_img, value_img = items
        scores = (
            jnp.einsum("qhd,khd->hqk", query_img, key_img, preferred_element_type=jnp.float32)
            * score_scale
        )
        row_max = jnp.max(scores, axis=-1, keepdims=True)
        expo = jnp.exp(scores - row_max)
        row_sum = jnp.sum(expo, axis=-1, keepdims=True)
        mixed = jnp.einsum(
            "hqk,khd->qhd",
            (expo / row_sum).astype(jnp.bfloat16),
            value_img,
            preferred_element_type=jnp.float32,
        )
        return (mixed, (row_max + jnp.log(row_sum))[:, :, 0])

    mixed_full, log_total = lax.map(attend, (query_low, key_heads, value_heads))
    attended = mixed_full.reshape(all_rows, model_width).astype(jnp.bfloat16)
    attn_out = product(attended, out_weight).reshape(images, tokens, model_width)
    middle = inputs + gate_in * attn_out
    normed_mid = normed(middle)
    hidden_mid = (
        (normed_mid * (1.0 + scale_mid) + shift_mid)
        .astype(jnp.bfloat16)
        .reshape(all_rows, model_width)
    )

    def feed(hidden_value):
        gate_up = product(hidden_value, gate_up_weight)
        return (gate_up[:, :hidden_units], gate_up[:, hidden_units:])

    gate_pre, up_pre = feed(hidden_mid)
    activ = (jax.nn.silu(gate_pre) * up_pre).astype(jnp.bfloat16)
    mlp_out = product(activ, down_weight).reshape(images, tokens, model_width)
    output = middle + gate_mid * mlp_out
    upstream = cotangent.reshape(images, tokens, model_width)
    gmid_grad = jnp.sum(upstream * mlp_out, axis=1)
    mlp_grad = (gate_mid * upstream).astype(jnp.bfloat16).reshape(all_rows, model_width)
    down_grad = product_lt(activ, mlp_grad)
    activ_grad = product_rt(mlp_grad, down_weight)
    gate_pre, up_pre = feed(hidden_mid)
    gu_grad = jnp.concatenate(
        [activ_grad * up_pre * silu_slope(gate_pre), activ_grad * jax.nn.silu(gate_pre)], axis=1
    ).astype(jnp.bfloat16)
    gateup_grad = product_lt(hidden_mid, gu_grad)
    mid_grad = product_rt(gu_grad, gate_up_weight).reshape(images, tokens, model_width)
    smid_grad = jnp.sum(mid_grad, axis=1)
    cmid_grad = jnp.sum(mid_grad * normed_mid, axis=1)
    middle_grad = upstream + norm_back(middle, mid_grad * (1.0 + scale_mid))
    gin_grad = jnp.sum(middle_grad * attn_out, axis=1)
    attn_grad = (gate_in * middle_grad).astype(jnp.bfloat16).reshape(all_rows, model_width)
    outw_grad = product_lt(attended, attn_grad)
    attended_grad = (
        product_rt(attn_grad, out_weight)
        .astype(jnp.bfloat16)
        .reshape(images, tokens, head_count, head_size)
    )
    row_delta = jnp.swapaxes(jnp.sum(attended_grad.astype(jnp.float32) * mixed_full, axis=-1), 1, 2)

    def score_parts(query_img, key_img, value_img, grad_img, total_img, delta_img):
        scores = (
            jnp.einsum("qhd,khd->hqk", query_img, key_img, preferred_element_type=jnp.float32)
            * score_scale
        )
        probs = jnp.exp(scores - total_img[:, :, None])
        prob_grad = jnp.einsum(
            "qhd,khd->hqk", grad_img, value_img, preferred_element_type=jnp.float32
        )
        score_grad = (probs * (prob_grad - delta_img[:, :, None])).astype(jnp.bfloat16)
        return (probs.astype(jnp.bfloat16), score_grad)

    def grads_all(items):
        query_img, key_img, value_img, grad_img, total_img, delta_img = items
        probs_low, score_grad = score_parts(
            query_img, key_img, value_img, grad_img, total_img, delta_img
        )
        query_part = (
            jnp.einsum("hqk,khd->qhd", score_grad, key_img, preferred_element_type=jnp.float32)
            * score_scale
        )
        key_part = (
            jnp.einsum("hqk,qhd->khd", score_grad, query_img, preferred_element_type=jnp.float32)
            * score_scale
        )
        value_part = jnp.einsum(
            "hqk,qhd->khd", probs_low, grad_img, preferred_element_type=jnp.float32
        )
        return (query_part, key_part.reshape(-1, model_width), value_part.reshape(-1, model_width))

    query_grad, key_full, value_full = lax.map(
        grads_all, (query_low, key_heads, value_heads, attended_grad, log_total, row_delta)
    )
    key_grad, value_grad = (
        lax.psum_scatter(
            key_full.astype(jnp.bfloat16), ("ty", "tx"), scatter_dimension=1, tiled=True
        ).astype(jnp.float32),
        lax.psum_scatter(
            value_full.astype(jnp.bfloat16), ("ty", "tx"), scatter_dimension=1, tiled=True
        ).astype(jnp.float32),
    )
    query_turned = rotate(query_grad, tables, -1.0)
    key_turned = rotate(key_grad.reshape(images, tokens, head_count, head_size), tables, -1.0)
    qgain_part = jnp.sum(query_turned * query_unit, axis=(0, 1, 2))
    kgain_part = jnp.sum(key_turned * key_unit, axis=(0, 1, 2))
    query_back = norm_back(query_raw, query_turned * query_gain).reshape(
        images, tokens, model_width
    )
    key_back = norm_back(key_raw, key_turned * key_gain).reshape(images, tokens, model_width)
    qkv_back = jnp.concatenate([query_back, key_back, value_grad], axis=-1).astype(jnp.bfloat16)
    qkv_back = qkv_back.reshape(all_rows, 3 * model_width)
    qkv_part = product_lt(hidden_in, qkv_back)
    in_back = product_rt(qkv_back, qkv_weight).reshape(images, tokens, model_width)
    sin_grad = jnp.sum(in_back, axis=1)
    cin_grad = jnp.sum(in_back * normed_in, axis=1)
    in_grad = middle_grad + norm_back(inputs, in_back * (1.0 + scale_in))
    mod_grad = jnp.concatenate(
        [sin_grad, cin_grad, gin_grad, smid_grad, cmid_grad, gmid_grad], axis=1
    )
    mod_cols = lax.psum_scatter(mod_grad, ("ty", "tx"), scatter_dimension=1, tiled=True)
    modw_part = jnp.dot(cond_act.astype(jnp.float32).T, mod_cols, precision=PRECISE)
    modb_part = jnp.sum(mod_cols, axis=0)
    act_grad = jnp.dot(mod_cols, mod_weight.astype(jnp.float32).T, precision=PRECISE)
    cond_grad = act_grad * silu_slope(condition)
    table_part = jnp.dot(onehot.T, cond_grad, precision=PRECISE)
    qkv_share, outw_share, gateup_share, down_share, table_share = (
        lax.psum_scatter(
            qkv_part.astype(jnp.bfloat16), ("ty", "tx"), scatter_dimension=0, tiled=True
        ).astype(jnp.float32),
        lax.psum_scatter(
            outw_grad.astype(jnp.bfloat16), ("ty", "tx"), scatter_dimension=0, tiled=True
        ).astype(jnp.float32),
        lax.psum_scatter(
            gateup_grad.astype(jnp.bfloat16), ("ty", "tx"), scatter_dimension=0, tiled=True
        ).astype(jnp.float32),
        lax.psum_scatter(
            down_grad.astype(jnp.bfloat16), ("ty", "tx"), scatter_dimension=0, tiled=True
        ).astype(jnp.float32),
        lax.psum_scatter(
            table_part.astype(jnp.bfloat16), ("ty", "tx"), scatter_dimension=0, tiled=True
        ).astype(jnp.float32),
    )
    qkv_total, outw_total, gateup_total, down_total, table_total = (
        lax.psum_scatter(
            qkv_share.astype(jnp.bfloat16), "img", scatter_dimension=1, tiled=True
        ).astype(jnp.float32),
        lax.psum_scatter(
            outw_share.astype(jnp.bfloat16), "img", scatter_dimension=1, tiled=True
        ).astype(jnp.float32),
        lax.psum_scatter(
            gateup_share.astype(jnp.bfloat16), "img", scatter_dimension=1, tiled=True
        ).astype(jnp.float32),
        lax.psum_scatter(
            down_share.astype(jnp.bfloat16), "img", scatter_dimension=1, tiled=True
        ).astype(jnp.float32),
        lax.psum_scatter(
            table_share.astype(jnp.bfloat16), "img", scatter_dimension=1, tiled=True
        ).astype(jnp.float32),
    )
    modw_total = lax.psum_scatter(
        modw_part.astype(jnp.bfloat16), "img", scatter_dimension=0, tiled=True
    ).astype(jnp.float32)
    modb_total = lax.psum(modb_part, "img")
    qgain_total, kgain_total = lax.psum((qgain_part, kgain_part), ("img", "ty", "tx"))
    return (
        output.reshape(block_in.shape),
        in_grad.reshape(block_in.shape),
        table_total,
        modw_total,
        modb_total,
        qkv_total,
        qgain_total,
        kgain_total,
        outw_total,
        gateup_total,
        down_total,
    )


def solution(mesh):
    return jax.shard_map(
        on_device,
        mesh=mesh,
        in_specs=(
            P("img", "ty", "tx", None),
            P("img"),
            P("img", "ty", "tx", None),
            P(),
            P(None, ("ty", "tx")),
            P(("ty", "tx")),
            P(),
            P(),
            P(),
            P(),
            P(),
            P(),
            P("img", "ty", "tx", None),
        ),
        out_specs=(
            P("img", "ty", "tx", None),
            P("img", "ty", "tx", None),
            P(("ty", "tx"), "img"),
            P("img", ("ty", "tx")),
            P(("ty", "tx")),
            P(("ty", "tx"), "img"),
            P(),
            P(),
            P(("ty", "tx"), "img"),
            P(("ty", "tx"), "img"),
            P(("ty", "tx"), "img"),
        ),
        check_vma=False,
    )
```

profile of v0, /device:TPU:0, one launch (start us, length us, event | category | flops | bytes accessed | tf_op | source)
XLA Modules:
  0.0 885.4 jit_solution(3208872247475456822)
XLA Ops:
  10.5 1.3 fusion.48
  12.4 2.2 convolution_reduce_fusion.2
  15.5 25.7 %all-reduce = f32[6912]{0:T(1024)S(1)} all-reduce(f32[6912]{0:T(1024)S(1)} %add_dynamic-update-slice_fusion), channel_id=2, replica_groups=mesh['img'=4,'ty'=4,'tx'=2] {'ty','tx'}, use_global_device_ids=true, to_apply=%add | all-reduce | flops 6912 | bytes 55296
  41.8 1.2 multiply_reduce_fusion.14
  43.1 4.7 convolution_bitcast_fusion
  47.9 1.2 copy-done.7
  50.2 2.2 copy.71
  55.3 1.3 fusion.33
  58.4 1.8 slice.220
  60.3 2.1 copy.70
  64.2 1.2 multiply_multiply_fusion.1
  65.4 1.6 fusion.22
  66.9 21.1 %all-gather.6.cloned.1.call-done = bf16[1,1024,1152]{1,2,0:T(8,128)(2,1)} async-done(((bf16[1,128,1152]{1,2,0:T(8,128)(2,1)}), bf16[1,1024,1152]{1,2,0:T(8,128)(2,1)}) %all-gather.6.cloned.1.call-update) | async-done | bytes 2359312 | tf_op jit(solution)/shard_map/all_gather | solution.py:119
  88.0 3.1 multiply_reduce_fusion
  91.2 1.9 fusion
  93.1 1.3 copy-done.2
  95.1 24.4 %all-gather.4.cloned.1.call-done = bf16[1,1024,1152]{2,1,0:T(8,128)(2,1)} async-done(((bf16[1,128,1152]{2,1,0:T(8,128)(2,1)}), bf16[1,1024,1152]{2,1,0:T(8,128)(2,1)}) %all-gather.4.cloned.1.call-update) | async-done | bytes 2359312 | tf_op jit(solution)/shard_map/all_gather | solution.py:122
  119.5 4.7 copy.69
  124.3 7.0 fusion.50
  132.7 4.1 fusion.45
  136.8 4.5 multiply_convert_fusion.4
  141.3 12.0 %multiply_reduce_fusion.3 = (f32[1152]{0:T(1024)}, f32[128]{0:T(128)S(1)}, f32[1152]{0:T(1024)}, f32[128,1152]{1,0:T(8,128)}) fusion(f32[128,1152]{1,0:T(8,128)S(1)} %get-tuple-element.128, f32[128]{0:T(128)S(1)} %add_rsqrt_fusion.3, f32[1152]{0:T(1024)S(1)} %get-tuple-element.113, bf16[1152,6144]{1,0:T(8,128)(2,1)} %param.23, ...), kind=kOutput, calls=%fused_computation.48 | convolution fusion | flops 1816114816 | bytes 16923136 | tf_op jit(solution)/shard_map/ik,jk->ij/dot_general | solution.py:55
  153.4 5.9 multiply_reduce_fusion.4
  160.1 1.6 convolution_convert_fusion.4
  164.1 5.7 multiply_convert_fusion
  171.8 8.6 copy.85
  180.4 4.1 copy.100
  184.6 5.2 fusion.7
  189.8 2.5 copy.81
  193.3 2.3 copy.80
  196.4 2.1 copy.76
  200.0 3.8 fusion.11
  206.4 20.8 %reduce-scatter.40.cloned.1.call-done = bf16[128,1152]{1,0:T(8,128)(2,1)} async-done(((bf16[1024,1152]{1,0:T(8,128)(2,1)}), bf16[128,1152]{1,0:T(8,128)(2,1)}) %reduce-scatter.40.cloned.1.call-update) | async-done | bytes 294928
  227.2 1.3 reshape_bitcast_fusion
  230.2 1.7 multiply_reduce_fusion.7
  231.9 2.2 copy.77
  235.2 2.5 multiply_reduce_fusion.1
  237.7 35.6 %reduce-scatter.26.cloned.1.call-done = bf16[1,128,1152]{2,1,0:T(8,128)(2,1)} async-done(((bf16[1,1024,1152]{2,1,0:T(8,128)(2,1)}), bf16[1,128,1152]{2,1,0:T(8,128)(2,1)}) %reduce-scatter.26.cloned.1.call-update) | async-done | bytes 294928 | tf_op jit(solution)/shard_map/reduce_scatter | solution.py:224
  273.3 7.2 multiply_reduce_fusion.5
  280.6 2.4 copy.87
  283.1 48.2 %reduce-scatter.42.cloned.1.call-done = f32[864,1]{1,0:T(8,128)} async-done(((f32[6912,1]{1,0:T(8,128)}), f32[864,1]{1,0:T(8,128)}) %reduce-scatter.42.cloned.1.call-update) | async-done | bytes 3472 | tf_op jit(solution)/shard_map/reshape.98
  331.3 2.6 convolution_reduce_fusion
  335.0 2.3 convolution_convert_fusion.3
  337.4 4.9 convolution_convert_fusion.2
  343.3 5.5 convolution_convert_fusion.1
  350.1 8.5 convolution_convert_fusion
  359.3 25.1 %all-reduce.5.cloned.1.call-done = bf16[32,1152]{1,0:T(8,128)(2,1)} async-done(((bf16[32,1152]{1,0:T(8,128)(2,1)}), bf16[32,1152]{1,0:T(8,128)(2,1)}) %all-reduce.5.cloned.1.call-update) | async-done | bytes 73744
  386.2 47.2 %reduce-scatter.32.cloned.1.call-done = bf16[144,1152]{1,0:T(8,128)(2,1)} async-done(((bf16[1152,1152]{1,0:T(8,128)(2,1)}), bf16[144,1152]{1,0:T(8,128)(2,1)}) %reduce-scatter.32.cloned.1.call-update) | async-done | bytes 331792 | tf_op jit(solution)/shard_map/reduce_scatter | solution.py:256
  433.4 2.0 copy.93
  435.7 1.6 multiply_convert_fusion.2
  437.4 65.0 %reduce-scatter.38.cloned.1.call-done = bf16[384,1152]{1,0:T(8,128)(2,1)} async-done(((bf16[3072,1152]{1,0:T(8,128)(2,1)}), bf16[384,1152]{1,0:T(8,128)(2,1)}) %reduce-scatter.38.cloned.1.call-update) | async-done | bytes 884752 | tf_op jit(solution)/shard_map/reduce_scatter | solution.py:262
  502.4 2.2 copy.95
  504.7 71.7 %reduce-scatter.30.cloned.1.call-done = bf16[144,3456]{1,0:T(8,128)(2,1)} async-done(((bf16[1152,3456]{1,0:T(8,128)(2,1)}), bf16[144,3456]{1,0:T(8,128)(2,1)}) %reduce-scatter.30.cloned.1.call-update) | async-done | bytes 995344 | tf_op jit(solution)/shard_map/reduce_scatter | solution.py:253
  576.4 2.6 copy.91
  579.1 101.5 %reduce-scatter.34.cloned.1.call-done = bf16[144,6144]{1,0:T(8,128)(2,1)} async-done(((bf16[1152,6144]{1,0:T(8,128)(2,1)}), bf16[144,6144]{1,0:T(8,128)(2,1)}) %reduce-scatter.34.cloned.1.call-update) | async-done | bytes 1769488 | tf_op jit(solution)/shard_map/reduce_scatter | solution.py:259
  680.9 39.4 %all-reduce.2 = (f32[72]{0:T(128)}, f32[72]{0:T(128)}) all-reduce(f32[72]{0:T(128)S(1)} %reduce_sum.233, f32[72]{0:T(128)S(1)} %reduce_sum.236), channel_id=1, replica_groups=mesh['img'=4,'ty'=4,'tx'=2] {'img','ty','tx'}, use_global_device_ids=true, to_apply=%region_28.29 | all-reduce | flops 144 | bytes 1152 | tf_op jit(solution)/shard_map/psum | solution.py:290
  721.3 11.1 %psum.21 = f32[864]{0:T(1024)} all-reduce(f32[864]{0:T(1024)S(1)} %bitcast_reduce_fusion), channel_id=1, replica_groups=mesh['img'=4,'ty'=4,'tx'=2] {'img'}, use_global_device_ids=true, to_apply=%region_23.24 | all-reduce | flops 864 | bytes 6912 | tf_op jit(solution)/shard_map/psum | solution.py:289
  735.9 34.5 %reduce-scatter.28.cloned.1.call-done = bf16[288,864]{1,0:T(8,128)(2,1)} async-done(((bf16[1152,864]{1,0:T(8,128)(2,1)}), bf16[288,864]{1,0:T(8,128)(2,1)}) %reduce-scatter.28.cloned.1.call-update) | async-done | bytes 497680 | tf_op jit(solution)/shard_map/reduce_scatter | solution.py:286
  770.4 2.1 convert_element_type.204
  772.5 24.7 %reduce-scatter.50.cloned.1.call-done = bf16[288,384]{1,0:T(8,128)(2,1)} async-done(((bf16[1152,384]{1,0:T(8,128)(2,1)}), bf16[288,384]{1,0:T(8,128)(2,1)}) %reduce-scatter.50.cloned.1.call-update) | async-done | bytes 221200
  799.2 37.7 %reduce-scatter.46.cloned.1.call-done = bf16[864,144]{1,0:T(8,128)(2,1)} async-done(((bf16[3456,144]{1,0:T(8,128)(2,1)}), bf16[864,144]{1,0:T(8,128)(2,1)}) %reduce-scatter.46.cloned.1.call-update) | async-done | bytes 248848
  836.9 1.2 copy.92
  838.9 37.7 %reduce-scatter.36.cloned.1.call-done = bf16[144,1536]{1,0:T(8,128)(2,1)} async-done(((bf16[144,6144]{1,0:T(8,128)(2,1)}), bf16[144,1536]{1,0:T(8,128)(2,1)}) %reduce-scatter.36.cloned.1.call-update) | async-done | bytes 442384 | tf_op jit(solution)/shard_map/reduce_scatter | solution.py:276
  876.6 2.0 convert_element_type.210
  (258 shorter events, 40.6 us)
Async XLA Ops:
  7.2 124.2 %copy-start = (bf16[1152,1152]{1,0:T(8,128)(2,1)S(1)}, bf16[1152,1152]{1,0:T(8,128)(2,1)}, u32[]{:S(2)}) copy-start(bf16[1152,1152]{1,0:T(8,128)(2,1)} %param.22) | copy-start | bytes 7962628
  7.2 35.9 %copy-start.4 = (f32[1,16,8,1152]{3,2,1,0:T(8,128)S(1)}, f32[1,16,8,1152]{3,2,1,0:T(8,128)}, u32[]{:S(2)}) copy-start(f32[1,16,8,1152]{3,2,1,0:T(8,128)} %param.13) | copy-start | bytes 1769476
  7.2 80.8 %all-gather.6.cloned.1.call-start = ((), (), s32[]{:S(2)}) async-start(), calls=%async_computation.14 | async-start | bytes 2654208 | tf_op jit(solution)/shard_map/all_gather | solution.py:119
  41.8 6.0 copy-start.37
  43.1 4.7 copy-start.64
  49.1 4.4 copy-start.69
  49.1 5.0 copy-start.67
  58.4 61.1 %all-gather.4.cloned.1.call-start = ((), (), s32[]{:S(2)}) async-start(), calls=%async_computation.13 | async-start | bytes 2654208 | tf_op jit(solution)/shard_map/all_gather | solution.py:122
  60.3 166.9 %reduce-scatter.40.cloned.1.call-start = ((), (), s32[]{:S(2)}) async-start(), calls=%async_computation.22 | async-start | bytes 2654208
  66.9 24.2 %copy-start.22 = (bf16[128,16,18]{0,2,1:T(8,128)(2,1)}, bf16[128,16,18]{0,2,1:T(8,128)(2,1)S(1)}, u32[]{:S(2)}) copy-start(bf16[128,16,18]{0,2,1:T(8,128)(2,1)S(1)} %get-tuple-element.144) | copy-start | bytes 221188
  66.9 24.2 %copy-start.24 = (bf16[128,16,18]{0,2,1:T(8,128)(2,1)}, bf16[128,16,18]{0,2,1:T(8,128)(2,1)S(1)}, u32[]{:S(2)}) copy-start(bf16[128,16,18]{0,2,1:T(8,128)(2,1)S(1)} %get-tuple-element.145) | copy-start | bytes 221188
  66.9 24.2 %copy-start.26 = (bf16[128,16,18]{0,2,1:T(8,128)(2,1)}, bf16[128,16,18]{0,2,1:T(8,128)(2,1)S(1)}, u32[]{:S(2)}) copy-start(bf16[128,16,18]{0,2,1:T(8,128)(2,1)S(1)} %get-tuple-element.158) | copy-start | bytes 221188
  94.5 29.7 %copy-start.61 = (f32[16,128]{1,0:T(8,128)}, f32[16,128]{1,0:T(8,128)S(1)}, u32[]{:S(2)}) copy-start(f32[16,128]{1,0:T(8,128)S(1)} %fusion) | copy-start | bytes 24580
  124.3 7.9 slice-start
  124.3 7.1 copy-start.39
  124.3 7.9 slice-start.1
  124.3 7.9 slice-start.2
  124.3 8.3 slice-start.3
  131.4 5.4 slice-start.4
  132.1 21.2 %copy-start.5 = (f32[128,1152]{1,0:T(8,128)}, f32[128,1152]{1,0:T(8,128)S(1)}, u32[]{:S(2)}) copy-start(f32[128,1152]{1,0:T(8,128)S(1)} %get-tuple-element.128) | copy-start | bytes 1769476
  132.1 21.2 %copy-start.62 = (f32[128]{0:T(128)}, f32[128]{0:T(128)S(1)}, u32[]{:S(2)}) copy-start(f32[128]{0:T(128)S(1)} %add_rsqrt_fusion.3) | copy-start | bytes 1540
  132.7 4.1 slice-start.5
  132.7 4.1 copy-start.19
  132.7 4.1 copy-start.51
  141.3 12.1 %copy-start.16 = (bf16[128,3072]{1,0:T(8,128)(2,1)}, bf16[128,3072]{1,0:T(8,128)(2,1)S(1)}, u32[]{:S(2)}) copy-start(bf16[128,3072]{1,0:T(8,128)(2,1)S(1)} %get-tuple-element.129) | copy-start | bytes 2359300
  141.3 12.1 %copy-start.18 = (bf16[128,3072]{1,0:T(8,128)(2,1)}, bf16[128,3072]{1,0:T(8,128)(2,1)S(1)}, u32[]{:S(2)}) copy-start(bf16[128,3072]{1,0:T(8,128)(2,1)S(1)} %get-tuple-element.130) | copy-start | bytes 2359300
  141.3 12.1 %copy-start.14 = (bf16[128,3072]{1,0:T(8,128)(2,1)}, bf16[128,3072]{1,0:T(8,128)(2,1)S(1)}, u32[]{:S(2)}) copy-start(bf16[128,3072]{1,0:T(8,128)(2,1)S(1)} %get-tuple-element.131) | copy-start | bytes 2359300
  164.0 5.7 copy-start.23
  164.1 5.7 copy-start.25
  164.1 5.7 copy-start.27
  164.1 5.7 copy-start.28
  184.5 88.7 %reduce-scatter.26.cloned.1.call-start = ((), (), s32[]{:S(2)}) async-start(), calls=%async_computation.15 | async-start | bytes 2654208 | tf_op jit(solution)/shard_map/reduce_scatter | solution.py:224
  192.4 6.2 copy-start.66
  192.4 6.9 copy-start.68
  192.4 7.6 copy-start.11
  192.4 138.9 %reduce-scatter.42.cloned.1.call-start = ((), (), s32[]{:S(2)}) async-start(), calls=%async_computation.23 | async-start | bytes 3981312 | tf_op jit(solution)/shard_map/reshape.98
  205.3 25.0 %copy-start.12 = (f32[1,128,1152]{1,2,0:T(8,128)S(1)}, f32[1,128,1152]{1,2,0:T(8,128)}, u32[]{:S(2)}) copy-start(f32[1,128,1152]{1,2,0:T(8,128)} %copy.71) | copy-start | bytes 1769476
  229.2 6.0 copy-start.8
  229.2 6.0 copy-start.59
  229.2 6.0 copy-start.60
  234.2 39.1 %copy-start.65 = (f32[128]{0:T(128)S(1)}, f32[128]{0:T(128)}, u32[]{:S(2)}) copy-start(f32[128]{0:T(128)} %copy-done.64) | copy-start | bytes 1540
  273.3 7.3 copy-start.58
  273.3 7.3 copy-start.56
  273.3 7.3 copy-start.55
  273.3 7.3 copy-start.57
  283.0 50.9 %copy-start.50 = (f32[1152]{0:T(1024)S(1)}, f32[1152]{0:T(1024)}, u32[]{:S(2)}) copy-start(f32[1152]{0:T(1024)} %copy-done.49) | copy-start | bytes 13828
  283.0 52.0 %copy-start.10 = (f32[128,1152]{1,0:T(8,128)S(1)}, f32[128,1152]{1,0:T(8,128)}, u32[]{:S(2)}) copy-start(f32[128,1152]{1,0:T(8,128)} %copy-done.9) | copy-start | bytes 1769476
  283.0 52.0 %copy-start.40 = (f32[1152]{0:T(1024)S(1)}, f32[1152]{0:T(1024)}, u32[]{:S(2)}) copy-start(f32[1152]{0:T(1024)} %get-tuple-element.116) | copy-start | bytes 13828
  283.0 101.4 %all-reduce.5.cloned.1.call-start = ((), (), s32[]{:S(2)}) async-start(), calls=%async_computation.28 | async-start | bytes 147456
  334.7 98.7 %reduce-scatter.32.cloned.1.call-start = ((), (), s32[]{:S(2)}) async-start(), calls=%async_computation.18 | async-start | bytes 2985984 | tf_op jit(solution)/shard_map/reduce_scatter | solution.py:256
  337.4 165.1 %reduce-scatter.38.cloned.1.call-start = ((), (), s32[]{:S(2)}) async-start(), calls=%async_computation.21 | async-start | bytes 7962624 | tf_op jit(solution)/shard_map/reduce_scatter | solution.py:262
  342.4 234.0 %reduce-scatter.30.cloned.1.call-start = ((), (), s32[]{:S(2)}) async-start(), calls=%async_computation.17 | async-start | bytes 8957952 | tf_op jit(solution)/shard_map/reduce_scatter | solution.py:253
  348.8 331.8 %reduce-scatter.34.cloned.1.call-start = ((), (), s32[]{:S(2)}) async-start(), calls=%async_computation.19 | async-start | bytes 15925248 | tf_op jit(solution)/shard_map/reduce_scatter | solution.py:259
  358.6 76.9 %copy-start.21 = (f32[864,1]{1,0:T(8,128)S(1)}, f32[864,1]{1,0:T(8,128)}, u32[]{:S(2)}) copy-start(f32[864,1]{1,0:T(8,128)} %reduce-scatter.42.cloned.1.call-done) | copy-start | bytes 10372
  358.6 77.1 %copy-start.54 = (f32[1152]{0:T(1024)S(1)}, f32[1152]{0:T(1024)}, u32[]{:S(2)}) copy-start(f32[1152]{0:T(1024)} %get-tuple-element.119) | copy-start | bytes 13828
  358.6 373.8 %reduce-scatter.44.cloned.1.call-start = ((), (), s32[]{:S(2)}) async-start(), calls=%async_computation.24 | async-start | bytes 368640
  386.1 348.0 %reduce-scatter.48.cloned.1.call-start = ((), (), s32[]{:S(2)}) async-start(), calls=%async_computation.26 | async-start | bytes 737280
  435.4 335.0 %reduce-scatter.28.cloned.1.call-start = ((), (), s32[]{:S(2)}) async-start(), calls=%async_computation.16 | async-start | bytes 2580480 | tf_op jit(solution)/shard_map/reduce_scatter | solution.py:286
  437.4 359.8 %reduce-scatter.50.cloned.1.call-start = ((), (), s32[]{:S(2)}) async-start(), calls=%async_computation.27 | async-start | bytes 1105920
  504.7 215.6 %copy-start.70 = (f32[128]{0:T(128)S(1)}, f32[128]{0:T(128)}, u32[]{:S(2)}) copy-start(f32[128]{0:T(128)} %get-tuple-element.108) | copy-start | bytes 1540
  504.7 215.6 %copy-start.29 = (f32[128,1152]{1,0:T(8,128)S(1)}, f32[128,1152]{1,0:T(8,128)}, u32[]{:S(2)}) copy-start(f32[128,1152]{1,0:T(8,128)} %get-tuple-element.181) | copy-start | bytes 1769476
  504.7 332.2 %reduce-scatter.46.cloned.1.call-start = ((), (), s32[]{:S(2)}) async-start(), calls=%async_computation.25 | async-start | bytes 2211840
  579.0 297.6 %reduce-scatter.36.cloned.1.call-start = ((), (), s32[]{:S(2)}) async-start(), calls=%async_computation.20 | async-start | bytes 2211840 | tf_op jit(solution)/shard_map/reduce_scatter | solution.py:276
  732.4 146.2 %copy-start.1 = (bf16[1152,1152]{1,0:T(8,128)(2,1)S(1)}, bf16[1152,1152]{1,0:T(8,128)(2,1)}, u32[]{:S(2)}) copy-start(bf16[1152,1152]{1,0:T(8,128)(2,1)} %param.22) | copy-start | bytes 7962628
  (29 other events, 61.5 us)
Sparse Core Ops, SparseCore 0:
  58.5 29.4 all-gather.5
  90.5 28.9 all-gather.3
  184.7 42.4 reduce-scatter.39
  230.8 42.4 reduce-scatter.25
  283.1 48.0 reduce-scatter.41
  334.8 49.5 all-reduce.4
  388.4 44.9 reduce-scatter.31
  436.9 65.5 reduce-scatter.37
  506.4 70.0 reduce-scatter.29
  579.9 100.7 reduce-scatter.33
  683.5 20.0 reduce-scatter.43
  706.3 20.2 reduce-scatter.47
  728.9 41.4 reduce-scatter.27
  773.2 23.8 reduce-scatter.49
  799.5 37.3 reduce-scatter.45
  839.1 37.4 reduce-scatter.35
where the time goes:
time: 892 us; the launch traced here: 885 us
  waiting for transfers between devices  595 us (67%)
  matrix products  93.7 us (11%)
  blocking collectives  76.2 us (9%)
  local copies, waits for them, and re-layouts  70.6 us (8%)
  other arithmetic  31.3 us (4%)
  between operations  17.3 us (2%)
    unnamed x22, waiting for transfers between devices  109 us
    reduce_scatter x1, waiting for transfers between devices, on_device(): lax.psum_scatter(gateup_grad.astype(jnp.bfloat16), ('ty', 'tx'), scatter_...  102 us
    reduce_scatter x1, waiting for transfers between devices, on_device(): lax.psum_scatter(qkv_part.astype(jnp.bfloat16), ('ty', 'tx'), scatter_dim...  71.7 us
    reduce_scatter x1, waiting for transfers between devices, on_device(): lax.psum_scatter(down_grad.astype(jnp.bfloat16), ('ty', 'tx'), scatter_di...  65 us
    another operation x1, waiting for transfers between devices  48.2 us
    reduce_scatter x1, waiting for transfers between devices, on_device(): lax.psum_scatter(outw_grad.astype(jnp.bfloat16), ('ty', 'tx'), scatter_di...  47.2 us
    unnamed x176, local copies, waits for them, and re-layouts  40.9 us
    psum x1, blocking collectives, on_device(): lax.psum((qgain_part, kgain_part), ('img', 'ty', 'tx'))  39.4 us
  transfers between devices with their start and end apart: 16, of which 14 were waited for; matrix products, arithmetic and copies ran while one was open for 10% of the time, Pallas kernels for 0%

commit v1 on v0

--- a/solution.py
+++ b/solution.py
@@ -8,6 +8,18 @@
 HD = 72
 EPS = 1e-06
 PRECISE = lax.Precision.HIGHEST
+
+
+def gather_by_bits(x, axis, dim):
+    ways, here = (lax.axis_size(axis), lax.axis_index(axis))
+    grown, reach = (x, 1)
+    while reach < ways:
+        theirs = lax.ppermute(grown, axis, [(d, d ^ reach) for d in range(ways)])
+        mine_first = jnp.concatenate([grown, theirs], axis=dim)
+        theirs_first = jnp.concatenate([theirs, grown], axis=dim)
+        grown = jnp.where(here & reach == 0, mine_first, theirs_first)
+        reach = 2 * reach
+    return grown
 
 
 def normed(value):
@@ -119,7 +131,7 @@
         lax.all_gather(
             key_low.reshape(images, tokens, model_width), ("ty", "tx"), axis=1, tiled=True
         ),
-        lax.all_gather(value_low, ("ty", "tx"), axis=1, tiled=True),
+        gather_by_bits(value_low, ("ty", "tx"), 1),
     )
     key_heads = keys_all.reshape(images, -1, head_count, head_size)
     value_heads = values_all.reshape(images, -1, head_count, head_size)

time: 892 us -> 887 us (level)
  waiting for transfers between devices: 595 us -> 576 us
    ppermute x0 -> x3, waiting for transfers between devices: none -> 26.1 us  [gather_by_bits(): theirs = lax.ppermute(grown, axis, [(d, d ^ reach) for d in range(ways)])]
    all_gather x1 -> x0, waiting for transfers between devices: 24.4 us -> none  [on_device(): lax.all_gather(value_low, ('ty', 'tx'), axis=1, tiled=True)]
    all_gather x1, waiting for transfers between devices: 21.1 us -> 0.01 us  [on_device(): lax.all_gather(key_low.reshape(images, tokens, model_width), ('ty', 'tx')...]
    unnamed x22 -> x21, waiting for transfers between devices: 109 us -> 108 us
    unnamed x176 -> x180, local copies, waits for them, and re-layouts: 40.9 us -> 41.4 us
  transfers between devices with their start and end apart: 16 -> 18, of which waited for: 14 -> 14; matrix products, arithmetic and copies ran while one was open for 10% -> 11% of each run, Pallas kernels for 0% -> 0%
where the time goes in v1:
time: 887 us; the launch traced here: 879 us
  waiting for transfers between devices  576 us (65%)
  matrix products  93.9 us (11%)
  blocking collectives  76.2 us (9%)
  local copies, waits for them, and re-layouts  73.9 us (8%)
  other arithmetic  38.7 us (4%)
  between operations  17.4 us (2%)
    unnamed x21, waiting for transfers between devices  108 us
    reduce_scatter x1, waiting for transfers between devices, on_device(): lax.psum_scatter(gateup_grad.astype(jnp.bfloat16), ('ty', 'tx'), scatter_...  102 us
    reduce_scatter x1, waiting for transfers between devices, on_device(): lax.psum_scatter(qkv_part.astype(jnp.bfloat16), ('ty', 'tx'), scatter_dim...  71.7 us
    reduce_scatter x1, waiting for transfers between devices, on_device(): lax.psum_scatter(down_grad.astype(jnp.bfloat16), ('ty', 'tx'), scatter_di...  65 us
    another operation x1, waiting for transfers between devices  48.2 us
    reduce_scatter x1, waiting for transfers between devices, on_device(): lax.psum_scatter(outw_grad.astype(jnp.bfloat16), ('ty', 'tx'), scatter_di...  47.1 us
    unnamed x180, local copies, waits for them, and re-layouts  41.4 us
    psum x1, blocking collectives, on_device(): lax.psum((qgain_part, kgain_part), ('img', 'ty', 'tx'))  39.5 us
  transfers between devices with their start and end apart: 18, of which 14 were waited for; matrix products, arithmetic and copies ran while one was open for 11% of the time, Pallas kernels for 0%

profile of v1, /device:TPU:0, one launch (start us, length us, event | category | flops | bytes accessed | tf_op | source)
XLA Modules:
  0.0 878.6 jit_solution(1776709323222877899)
XLA Ops:
  10.5 1.3 fusion.51
  12.4 2.2 convolution_reduce_fusion.2
  15.5 25.7 %all-reduce = f32[6912]{0:T(1024)S(1)} all-reduce(f32[6912]{0:T(1024)S(1)} %add_dynamic-update-slice_fusion), channel_id=2, replica_groups=mesh['img'=4,'ty'=4,'tx'=2] {'ty','tx'}, use_global_device_ids=true, to_apply=%add | all-reduce | flops 6912 | bytes 55296
  42.1 4.7 convolution_bitcast_fusion
  46.8 1.2 copy-done.7
  49.1 2.2 copy.86
  54.2 1.3 fusion.34
  58.6 9.0 %collective-permute-done = bf16[1,128,1152]{2,1,0:T(8,128)(2,1)} collective-permute-done((bf16[1,128,1152]{2,1,0:T(8,128)(2,1)S(1)}, bf16[1,128,1152]{2,1,0:T(8,128)(2,1)}, u32[]{:S(2)}, u32[]{:S(2)}) %collective-permute-start) | collective-permute-done | bytes 294944 | tf_op jit(solution)/shard_map/ppermute | solution.py:17
  72.0 1.5 maximum_select_fusion.2
  75.5 2.2 copy.85
  80.6 1.6 fusion.23
  82.2 1.8 copy.82
  84.1 2.1 maximum_select_fusion.3
  86.1 2.1 copy.83
  88.3 3.1 maximum_select_fusion.1
  91.4 17.1 %collective-permute-done.2 = bf16[1,512,1152]{2,1,0:T(8,128)(2,1)} collective-permute-done((bf16[1,512,1152]{2,1,0:T(8,128)(2,1)}, bf16[1,512,1152]{2,1,0:T(8,128)(2,1)}, u32[]{:S(2)}, u32[]{:S(2)}) %collective-permute-start.2) | collective-permute-done | bytes 1179680 | tf_op jit(solution)/shard_map/ppermute | solution.py:17
  108.5 2.4 copy.84
  110.9 3.1 multiply_reduce_fusion
  114.1 1.9 fusion
  117.7 4.3 fusion.53
  122.9 8.0 fusion.48
  130.9 2.5 multiply_convert_fusion.4
  133.4 12.0 %multiply_reduce_fusion.3 = (f32[1152]{0:T(1024)}, f32[128]{0:T(128)S(1)}, f32[1152]{0:T(1024)}, f32[128,1152]{1,0:T(8,128)}) fusion(f32[128,1152]{1,0:T(8,128)S(1)} %get-tuple-element.128, f32[128]{0:T(128)S(1)} %add_rsqrt_fusion.3, f32[1152]{0:T(1024)S(1)} %get-tuple-element.113, bf16[1152,6144]{1,0:T(8,128)(2,1)} %param.23, ...), kind=kOutput, calls=%fused_computation.55 | convolution fusion | flops 1816114816 | bytes 16923136 | tf_op jit(solution)/shard_map/ik,jk->ij/dot_general | solution.py:67
  145.5 5.9 multiply_reduce_fusion.4
  152.2 1.6 convolution_convert_fusion.4
  156.2 6.7 multiply_convert_fusion
  164.9 8.6 copy.100
  173.5 4.1 copy.115
  177.7 5.2 fusion.7
  182.9 2.5 copy.96
  187.0 2.1 copy.95
  190.0 2.2 copy.91
  193.6 3.8 fusion.11
  200.0 20.2 %reduce-scatter.40.cloned.1.call-done = bf16[128,1152]{1,0:T(8,128)(2,1)} async-done(((bf16[1024,1152]{1,0:T(8,128)(2,1)}), bf16[128,1152]{1,0:T(8,128)(2,1)}) %reduce-scatter.40.cloned.1.call-update) | async-done | bytes 294928
  220.3 1.3 reshape_bitcast_fusion
  222.5 1.8 multiply_reduce_fusion.7
  224.3 2.2 copy.92
  227.6 2.4 multiply_reduce_fusion.1
  230.0 36.5 %reduce-scatter.26.cloned.1.call-done = bf16[1,128,1152]{2,1,0:T(8,128)(2,1)} async-done(((bf16[1,1024,1152]{2,1,0:T(8,128)(2,1)}), bf16[1,128,1152]{2,1,0:T(8,128)(2,1)}) %reduce-scatter.26.cloned.1.call-update) | async-done | bytes 294928 | tf_op jit(solution)/shard_map/reduce_scatter | solution.py:236
  266.5 7.2 multiply_reduce_fusion.5
  273.8 2.4 copy.102
  276.3 48.2 %reduce-scatter.42.cloned.1.call-done = f32[864,1]{1,0:T(8,128)} async-done(((f32[6912,1]{1,0:T(8,128)}), f32[864,1]{1,0:T(8,128)}) %reduce-scatter.42.cloned.1.call-update) | async-done | bytes 3472 | tf_op jit(solution)/shard_map/reshape.98
  324.5 2.6 convolution_reduce_fusion
  328.0 2.3 convolution_convert_fusion.3
  330.7 4.9 convolution_convert_fusion.2
  336.6 5.5 convolution_convert_fusion.1
  343.3 8.5 convolution_convert_fusion
  352.6 25.1 %all-reduce.5.cloned.1.call-done = bf16[32,1152]{1,0:T(8,128)(2,1)} async-done(((bf16[32,1152]{1,0:T(8,128)(2,1)}), bf16[32,1152]{1,0:T(8,128)(2,1)}) %all-reduce.5.cloned.1.call-update) | async-done | bytes 73744
  379.4 47.1 %reduce-scatter.32.cloned.1.call-done = bf16[144,1152]{1,0:T(8,128)(2,1)} async-done(((bf16[1152,1152]{1,0:T(8,128)(2,1)}), bf16[144,1152]{1,0:T(8,128)(2,1)}) %reduce-scatter.32.cloned.1.call-update) | async-done | bytes 331792 | tf_op jit(solution)/shard_map/reduce_scatter | solution.py:268
  426.4 2.0 copy.108
  428.8 1.7 multiply_convert_fusion.2
  430.5 65.0 %reduce-scatter.38.cloned.1.call-done = bf16[384,1152]{1,0:T(8,128)(2,1)} async-done(((bf16[3072,1152]{1,0:T(8,128)(2,1)}), bf16[384,1152]{1,0:T(8,128)(2,1)}) %reduce-scatter.38.cloned.1.call-update) | async-done | bytes 884752 | tf_op jit(solution)/shard_map/reduce_scatter | solution.py:274
  495.5 2.2 copy.110
  497.8 71.7 %reduce-scatter.30.cloned.1.call-done = bf16[144,3456]{1,0:T(8,128)(2,1)} async-done(((bf16[1152,3456]{1,0:T(8,128)(2,1)}), bf16[144,3456]{1,0:T(8,128)(2,1)}) %reduce-scatter.30.cloned.1.call-update) | async-done | bytes 995344 | tf_op jit(solution)/shard_map/reduce_scatter | solution.py:265
  569.5 2.6 copy.106
  572.1 101.7 %reduce-scatter.34.cloned.1.call-done = bf16[144,6144]{1,0:T(8,128)(2,1)} async-done(((bf16[1152,6144]{1,0:T(8,128)(2,1)}), bf16[144,6144]{1,0:T(8,128)(2,1)}) %reduce-scatter.34.cloned.1.call-update) | async-done | bytes 1769488 | tf_op jit(solution)/shard_map/reduce_scatter | solution.py:271
  674.1 39.5 %all-reduce.2 = (f32[72]{0:T(128)}, f32[72]{0:T(128)}) all-reduce(f32[72]{0:T(128)S(1)} %reduce_sum.233, f32[72]{0:T(128)S(1)} %reduce_sum.236), channel_id=1, replica_groups=mesh['img'=4,'ty'=4,'tx'=2] {'img','ty','tx'}, use_global_device_ids=true, to_apply=%region_28.29 | all-reduce | flops 144 | bytes 1152 | tf_op jit(solution)/shard_map/psum | solution.py:302
  714.6 11.0 %psum.21 = f32[864]{0:T(1024)} all-reduce(f32[864]{0:T(1024)S(1)} %bitcast_reduce_fusion), channel_id=1, replica_groups=mesh['img'=4,'ty'=4,'tx'=2] {'img'}, use_global_device_ids=true, to_apply=%region_23.24 | all-reduce | flops 864 | bytes 6912 | tf_op jit(solution)/shard_map/psum | solution.py:301
  729.0 34.4 %reduce-scatter.28.cloned.1.call-done = bf16[288,864]{1,0:T(8,128)(2,1)} async-done(((bf16[1152,864]{1,0:T(8,128)(2,1)}), bf16[288,864]{1,0:T(8,128)(2,1)}) %reduce-scatter.28.cloned.1.call-update) | async-done | bytes 497680 | tf_op jit(solution)/shard_map/reduce_scatter | solution.py:298
  763.4 2.2 convert_element_type.204
  765.6 24.7 %reduce-scatter.50.cloned.1.call-done = bf16[288,384]{1,0:T(8,128)(2,1)} async-done(((bf16[1152,384]{1,0:T(8,128)(2,1)}), bf16[288,384]{1,0:T(8,128)(2,1)}) %reduce-scatter.50.cloned.1.call-update) | async-done | bytes 221200
  792.4 37.7 %reduce-scatter.46.cloned.1.call-done = bf16[864,144]{1,0:T(8,128)(2,1)} async-done(((bf16[3456,144]{1,0:T(8,128)(2,1)}), bf16[864,144]{1,0:T(8,128)(2,1)}) %reduce-scatter.46.cloned.1.call-update) | async-done | bytes 248848
  832.1 37.7 %reduce-scatter.36.cloned.1.call-done = bf16[144,1536]{1,0:T(8,128)(2,1)} async-done(((bf16[144,6144]{1,0:T(8,128)(2,1)}), bf16[144,1536]{1,0:T(8,128)(2,1)}) %reduce-scatter.36.cloned.1.call-update) | async-done | bytes 442384 | tf_op jit(solution)/shard_map/reduce_scatter | solution.py:288
  869.8 2.0 convert_element_type.210
  (273 shorter events, 50.7 us)
Async XLA Ops:
  7.2 114.9 %copy-start = (bf16[1152,1152]{1,0:T(8,128)(2,1)S(1)}, bf16[1152,1152]{1,0:T(8,128)(2,1)}, u32[]{:S(2)}) copy-start(bf16[1152,1152]{1,0:T(8,128)(2,1)} %param.22) | copy-start | bytes 7962628
  7.2 34.6 %copy-start.3 = (f32[1,16,8,1152]{3,2,1,0:T(8,128)S(1)}, f32[1,16,8,1152]{3,2,1,0:T(8,128)}, u32[]{:S(2)}) copy-start(f32[1,16,8,1152]{3,2,1,0:T(8,128)} %param.13) | copy-start | bytes 1769476
  7.2 103.7 %all-gather.3.cloned.1.call-start = ((), (), s32[]{:S(2)}) async-start(), calls=%async_computation.13 | async-start | bytes 2654208 | tf_op jit(solution)/shard_map/all_gather | solution.py:131
  41.8 4.9 copy-start.43
  42.1 4.7 copy-start.70
  48.0 5.0 copy-start.73
  57.3 162.9 %reduce-scatter.40.cloned.1.call-start = ((), (), s32[]{:S(2)}) async-start(), calls=%async_computation.21 | async-start | bytes 2654208
  58.5 9.1 %collective-permute-start = (bf16[1,128,1152]{2,1,0:T(8,128)(2,1)S(1)}, bf16[1,128,1152]{2,1,0:T(8,128)(2,1)}, u32[]{:S(2)}, u32[]{:S(2)}) collective-permute-start(bf16[1,128,1152]{2,1,0:T(8,128)(2,1)S(1)} %slice.220), channel_id=1, source_target_pairs={{0,1},{1,0},{2,3},{3,2},{4,5},{5,4},{6,7},{7,6},{8,9},{9,8},{10,11... | collective-permute-start | bytes 884744 | tf_op jit(solution)/shard_map/ppermute | solution.py:17
  68.8 2.4 collective-permute-start.1
  73.5 35.0 %collective-permute-start.2 = (bf16[1,512,1152]{2,1,0:T(8,128)(2,1)}, bf16[1,512,1152]{2,1,0:T(8,128)(2,1)}, u32[]{:S(2)}, u32[]{:S(2)}) collective-permute-start(bf16[1,512,1152]{2,1,0:T(8,128)(2,1)} %maximum_select_fusion.2), channel_id=1, source_target_pairs={{0,4},{1,5},{2,6},{3,7},{4,0},{5,1},{6,2},{7,3},{8,12},{9,13},{10,... | collective-permute-start | bytes 3538952 | tf_op jit(solution)/shard_map/ppermute | solution.py:17
  75.5 8.6 copy-start.25
  88.3 22.6 %copy-start.26 = (bf16[128,16,18]{0,2,1:T(8,128)(2,1)S(1)}, bf16[128,16,18]{0,2,1:T(8,128)(2,1)}, u32[]{:S(2)}) copy-start(bf16[128,16,18]{0,2,1:T(8,128)(2,1)} %get-tuple-element.144) | copy-start | bytes 221188
  88.3 22.6 %copy-start.28 = (bf16[128,16,18]{0,2,1:T(8,128)(2,1)S(1)}, bf16[128,16,18]{0,2,1:T(8,128)(2,1)}, u32[]{:S(2)}) copy-start(bf16[128,16,18]{0,2,1:T(8,128)(2,1)} %get-tuple-element.145) | copy-start | bytes 221188
  88.3 22.6 %copy-start.30 = (bf16[128,16,18]{0,2,1:T(8,128)(2,1)S(1)}, bf16[128,16,18]{0,2,1:T(8,128)(2,1)}, u32[]{:S(2)}) copy-start(bf16[128,16,18]{0,2,1:T(8,128)(2,1)} %get-tuple-element.158) | copy-start | bytes 221188
  122.1 8.8 %slice-start = ((s8[7077888]{0:T(1024)(128)(4,1)}), s8[4194304]{0:T(1024)(128)(4,1)S(1)}, s32[]{:S(2)}) async-start(s8[7077888]{0:T(1024)(128)(4,1)} %bitcast.140), calls=%async_computation.28 | async-start | bytes 8388608
  122.8 22.6 %copy-start.5 = (f32[128,1152]{1,0:T(8,128)}, f32[128,1152]{1,0:T(8,128)S(1)}, u32[]{:S(2)}) copy-start(f32[128,1152]{1,0:T(8,128)S(1)} %get-tuple-element.128) | copy-start | bytes 1769476
  122.8 22.6 %copy-start.68 = (f32[128]{0:T(128)}, f32[128]{0:T(128)S(1)}, u32[]{:S(2)}) copy-start(f32[128]{0:T(128)S(1)} %add_rsqrt_fusion.3) | copy-start | bytes 1540
  122.8 8.0 slice-start.1
  122.9 8.0 copy-start.19
  122.9 8.0 copy-start.59
  133.4 12.1 %copy-start.16 = (bf16[128,3072]{1,0:T(8,128)(2,1)}, bf16[128,3072]{1,0:T(8,128)(2,1)S(1)}, u32[]{:S(2)}) copy-start(bf16[128,3072]{1,0:T(8,128)(2,1)S(1)} %get-tuple-element.129) | copy-start | bytes 2359300
  133.4 12.1 %copy-start.18 = (bf16[128,3072]{1,0:T(8,128)(2,1)}, bf16[128,3072]{1,0:T(8,128)(2,1)S(1)}, u32[]{:S(2)}) copy-start(bf16[128,3072]{1,0:T(8,128)(2,1)S(1)} %get-tuple-element.130) | copy-start | bytes 2359300
  133.4 12.1 %copy-start.14 = (bf16[128,3072]{1,0:T(8,128)(2,1)}, bf16[128,3072]{1,0:T(8,128)(2,1)S(1)}, u32[]{:S(2)}) copy-start(bf16[128,3072]{1,0:T(8,128)(2,1)S(1)} %get-tuple-element.131) | copy-start | bytes 2359300
  156.2 6.7 copy-start.27
  156.2 6.7 copy-start.29
  156.2 6.7 copy-start.31
  156.2 6.7 copy-start.32
  177.6 88.8 %reduce-scatter.26.cloned.1.call-start = ((), (), s32[]{:S(2)}) async-start(), calls=%async_computation.14 | async-start | bytes 2654208 | tf_op jit(solution)/shard_map/reduce_scatter | solution.py:236
  185.5 6.7 copy-start.72
  185.5 7.4 copy-start.74
  185.5 8.0 copy-start.11
  185.5 139.0 %reduce-scatter.42.cloned.1.call-start = ((), (), s32[]{:S(2)}) async-start(), calls=%async_computation.22 | async-start | bytes 3981312 | tf_op jit(solution)/shard_map/reshape.98
  198.9 23.4 %copy-start.36 = (f32[128,18]{0,1:T(8,128)S(1)}, f32[128,18]{0,1:T(8,128)}, u32[]{:S(2)}) copy-start(f32[128,18]{0,1:T(8,128)} %copy-done.34) | copy-start | bytes 27652
  198.9 23.4 %copy-start.39 = (f32[128,18]{0,1:T(8,128)S(1)}, f32[128,18]{0,1:T(8,128)}, u32[]{:S(2)}) copy-start(f32[128,18]{0,1:T(8,128)} %copy-done.37) | copy-start | bytes 27652
  198.9 23.4 %copy-start.52 = (f32[128,18]{0,1:T(8,128)S(1)}, f32[128,18]{0,1:T(8,128)}, u32[]{:S(2)}) copy-start(f32[128,18]{0,1:T(8,128)} %get-tuple-element.162) | copy-start | bytes 27652
  198.9 23.4 %copy-start.54 = (f32[128,18]{0,1:T(8,128)S(1)}, f32[128,18]{0,1:T(8,128)}, u32[]{:S(2)}) copy-start(f32[128,18]{0,1:T(8,128)} %get-tuple-element.172) | copy-start | bytes 27652
  200.0 22.4 %copy-start.12 = (f32[1,128,1152]{1,2,0:T(8,128)S(1)}, f32[1,128,1152]{1,2,0:T(8,128)}, u32[]{:S(2)}) copy-start(f32[1,128,1152]{1,2,0:T(8,128)} %copy.86) | copy-start | bytes 1769476
  222.4 5.1 copy-start.8
  222.5 5.1 copy-start.66
  222.5 5.1 copy-start.67
  227.6 38.9 %copy-start.71 = (f32[128]{0:T(128)S(1)}, f32[128]{0:T(128)}, u32[]{:S(2)}) copy-start(f32[128]{0:T(128)} %copy-done.70) | copy-start | bytes 1540
  266.5 7.3 copy-start.65
  266.5 7.3 copy-start.63
  266.5 7.3 copy-start.62
  266.5 7.3 copy-start.64
  276.2 50.9 %copy-start.58 = (f32[1152]{0:T(1024)S(1)}, f32[1152]{0:T(1024)}, u32[]{:S(2)}) copy-start(f32[1152]{0:T(1024)} %copy-done.57) | copy-start | bytes 13828
  276.2 51.8 %copy-start.10 = (f32[128,1152]{1,0:T(8,128)S(1)}, f32[128,1152]{1,0:T(8,128)}, u32[]{:S(2)}) copy-start(f32[128,1152]{1,0:T(8,128)} %copy-done.9) | copy-start | bytes 1769476
  276.2 51.8 %copy-start.46 = (f32[1152]{0:T(1024)S(1)}, f32[1152]{0:T(1024)}, u32[]{:S(2)}) copy-start(f32[1152]{0:T(1024)} %get-tuple-element.116) | copy-start | bytes 13828
  276.2 101.4 %all-reduce.5.cloned.1.call-start = ((), (), s32[]{:S(2)}) async-start(), calls=%async_computation.27 | async-start | bytes 147456
  327.9 98.5 %reduce-scatter.32.cloned.1.call-start = ((), (), s32[]{:S(2)}) async-start(), calls=%async_computation.17 | async-start | bytes 2985984 | tf_op jit(solution)/shard_map/reduce_scatter | solution.py:268
  330.4 165.1 %reduce-scatter.38.cloned.1.call-start = ((), (), s32[]{:S(2)}) async-start(), calls=%async_computation.20 | async-start | bytes 7962624 | tf_op jit(solution)/shard_map/reduce_scatter | solution.py:274
  335.6 233.9 %reduce-scatter.30.cloned.1.call-start = ((), (), s32[]{:S(2)}) async-start(), calls=%async_computation.16 | async-start | bytes 8957952 | tf_op jit(solution)/shard_map/reduce_scatter | solution.py:265
  342.0 331.8 %reduce-scatter.34.cloned.1.call-start = ((), (), s32[]{:S(2)}) async-start(), calls=%async_computation.18 | async-start | bytes 15925248 | tf_op jit(solution)/shard_map/reduce_scatter | solution.py:271
  351.8 76.7 %copy-start.22 = (f32[864,1]{1,0:T(8,128)S(1)}, f32[864,1]{1,0:T(8,128)}, u32[]{:S(2)}) copy-start(f32[864,1]{1,0:T(8,128)} %reduce-scatter.42.cloned.1.call-done) | copy-start | bytes 10372
  351.8 76.9 %copy-start.61 = (f32[1152]{0:T(1024)S(1)}, f32[1152]{0:T(1024)}, u32[]{:S(2)}) copy-start(f32[1152]{0:T(1024)} %get-tuple-element.119) | copy-start | bytes 13828
  351.9 373.8 %reduce-scatter.44.cloned.1.call-start = ((), (), s32[]{:S(2)}) async-start(), calls=%async_computation.23 | async-start | bytes 368640
  379.3 348.0 %reduce-scatter.48.cloned.1.call-start = ((), (), s32[]{:S(2)}) async-start(), calls=%async_computation.25 | async-start | bytes 737280
  428.5 334.9 %reduce-scatter.28.cloned.1.call-start = ((), (), s32[]{:S(2)}) async-start(), calls=%async_computation.15 | async-start | bytes 2580480 | tf_op jit(solution)/shard_map/reduce_scatter | solution.py:298
  430.5 359.9 %reduce-scatter.50.cloned.1.call-start = ((), (), s32[]{:S(2)}) async-start(), calls=%async_computation.26 | async-start | bytes 1105920
  497.7 332.4 %reduce-scatter.46.cloned.1.call-start = ((), (), s32[]{:S(2)}) async-start(), calls=%async_computation.24 | async-start | bytes 2211840
  572.1 141.6 %copy-start.76 = (f32[128]{0:T(128)S(1)}, f32[128]{0:T(128)}, u32[]{:S(2)}) copy-start(f32[128]{0:T(128)} %get-tuple-element.108) | copy-start | bytes 1540
  572.1 141.6 %copy-start.33 = (f32[128,1152]{1,0:T(8,128)S(1)}, f32[128,1152]{1,0:T(8,128)}, u32[]{:S(2)}) copy-start(f32[128,1152]{1,0:T(8,128)} %get-tuple-element.181) | copy-start | bytes 1769476
  572.1 297.7 %reduce-scatter.36.cloned.1.call-start = ((), (), s32[]{:S(2)}) async-start(), calls=%async_computation.19 | async-start | bytes 2211840 | tf_op jit(solution)/shard_map/reduce_scatter | solution.py:288
  763.4 108.4 %copy-start.1 = (bf16[1152,1152]{1,0:T(8,128)(2,1)S(1)}, bf16[1152,1152]{1,0:T(8,128)(2,1)}, u32[]{:S(2)}) copy-start(bf16[1152,1152]{1,0:T(8,128)(2,1)} %param.22) | copy-start | bytes 7962628
  (33 other events, 73.4 us)
Sparse Core Ops, SparseCore 0:
  57.4 35.8 all-gather.2
  177.8 42.4 reduce-scatter.39
  224.0 42.4 reduce-scatter.25
  276.4 48.0 reduce-scatter.41
  328.0 49.5 all-reduce.4
  381.4 44.9 reduce-scatter.31
  430.0 65.4 reduce-scatter.37
  499.4 70.0 reduce-scatter.29
  573.1 100.7 reduce-scatter.33
  676.5 20.0 reduce-scatter.43
  699.5 20.1 reduce-scatter.47
  721.9 41.4 reduce-scatter.27
  766.4 23.8 reduce-scatter.49
  792.6 37.3 reduce-scatter.45
  832.2 37.5 reduce-scatter.35
